TPU v7x, 32 devices: a whole 2x2x4 slice. The times are simulated.
32 devices in a mesh: seq: 16 (over z, y, core), head: 2 (over x).
Axes of the slice: x: 2, y: 2, z: 4, core: 2. Of those that a mesh axis runs over, the one named last changes fastest.
Arguments:
- queries: bfloat16 [4, 64, 64, 128], P(None, None, 'head'), may hold values from -15 to 15
- new_keys: bfloat16 [4, 64, 8, 128], P(None, None, 'head'), may hold values from -16 to 16
- new_values: bfloat16 [4, 64, 8, 128], P(None, None, 'head'), may hold values from -6 to 6
- cache_keys: bfloat16 [4, 32768, 8, 128], P(None, 'seq', 'head'), may hold values from -6 to 6
- cache_values: bfloat16 [4, 32768, 8, 128], P(None, 'seq', 'head'), may hold values from -6 to 6
- parents: int32 [4, 64], replicated, may hold values from 0 to 63, as said below
- kv_lengths: int32 [4], replicated, may hold values from 1 to 32768
- out_weight: bfloat16 [8192, 8192], P('head', 'seq'), may hold values from -0.5 to 0.5
Outputs:
- mixed: bfloat16 [256, 8192], P('head', 'seq')
Inputs may be any that keep to these rules, and one draw needn't show every extreme that they name: parents[r, 0] = 0 for the root; for i >= 1, parents[r, i] < i.
All inputs are finite; a program needn't handle non-finite values.
Results may differ from a plain program's by a relative error of at most 0.0045.
Values may be sent and summed in bfloat16 or wider, within the bound.
A program may use at most 128 MiB of HBM per device.

v0:
```python
import math
import jax
import jax.numpy as jnp
from jax import lax
from jax.sharding import PartitionSpec as P

lowest = -1e30


def ancestors(parent_row):
    tree_size = parent_row.shape[0]
    indices = jnp.arange(tree_size, dtype=jnp.int32)
    parent_link = (parent_row[:, None] == indices[None, :]).astype(jnp.float32)
    itself = (indices[:, None] == indices[None, :]).astype(jnp.float32)
    reached = jnp.maximum(parent_link, itself)
    for repeat in range(max(1, (tree_size - 1).bit_length())):
        reached = jnp.minimum(jnp.dot(reached, reached, precision=lax.Precision.HIGHEST), 1.0)
    return reached


def partial_scores(query_rows, keys, values, allowed, score_scale):
    scores = (
        jnp.einsum("kqd,pkd->kqp", query_rows, keys, preferred_element_type=jnp.float32)
        * score_scale
    )
    scores = jnp.where(allowed, scores, lowest)
    maxima = jnp.max(scores, axis=-1)
    weights = jnp.where(allowed, jnp.exp(scores - maxima[..., None]), 0.0)
    totals = jnp.sum(weights, axis=-1)
    weighted = jnp.einsum(
        "kqp,pkd->kqd", weights.astype(jnp.bfloat16), values, preferred_element_type=jnp.float32
    )
    return (maxima, totals, weighted)


def body(queries, new_keys, new_values, cache_keys, cache_values, parents, kv_lengths, out_weight):
    requests, tree_size, heads, head_size = queries.shape
    kv_heads = new_keys.shape[2]
    group_size = heads // kv_heads
    block_size = cache_keys.shape[1]
    score_scale = 1.0 / math.sqrt(head_size)
    tokens = requests * tree_size
    positions = lax.axis_index("seq") * block_size + jnp.arange(block_size, dtype=jnp.int32)

    def token_order(maxima, totals, weighted):
        maxima = (
            maxima.reshape(kv_heads, tree_size, group_size)
            .transpose(1, 0, 2)
            .reshape(tree_size, heads)
        )
        totals = (
            totals.reshape(kv_heads, tree_size, group_size)
            .transpose(1, 0, 2)
            .reshape(tree_size, heads)
        )
        weighted = weighted.reshape(kv_heads, tree_size, group_size, head_size).transpose(
            1, 0, 2, 3
        )
        return (maxima, totals, weighted.reshape(tree_size, heads, head_size))

    def one_request(request_items):
        query, tree_keys, tree_values, past_keys, past_values, parent_row, length = request_items
        query_rows = query.reshape(tree_size, kv_heads, group_size, head_size).transpose(1, 0, 2, 3)
        query_rows = query_rows.reshape(kv_heads, tree_size * group_size, head_size)
        cache_max, cache_tot, cache_acc = partial_scores(
            query_rows, past_keys, past_values, positions < length, score_scale
        )
        tree_allowed = jnp.repeat(ancestors(parent_row), group_size, axis=0) > 0.5
        tree_max, tree_tot, tree_acc = partial_scores(
            query_rows, tree_keys, tree_values, tree_allowed, score_scale
        )
        return (
            token_order(cache_max, cache_tot, cache_acc),
            token_order(tree_max, tree_tot, tree_acc),
        )

    cache_part, tree_part = lax.map(
        one_request, (queries, new_keys, new_values, cache_keys, cache_values, parents, kv_lengths)
    )
    cache_max = cache_part[0].reshape(tokens, heads)
    cache_tot = cache_part[1].reshape(tokens, heads)
    cache_acc = cache_part[2].reshape(tokens, heads, head_size)
    tree_max = tree_part[0].reshape(tokens, heads)
    tree_tot = tree_part[1].reshape(tokens, heads)
    tree_acc = tree_part[2].reshape(tokens, heads, head_size)
    overall = lax.pmax(cache_max, "seq")
    overall = jnp.maximum(overall, tree_max)
    factor = jnp.exp(cache_max - overall)
    shared_acc, shared_tot = (
        lax.psum_scatter(cache_acc * factor[..., None], "seq", scatter_dimension=0, tiled=True),
        lax.psum_scatter(cache_tot * factor, "seq", scatter_dimension=0, tiled=True),
    )
    row_count = tokens // lax.axis_size("seq")
    first_row = lax.axis_index("seq") * row_count

    def take_rows(array):
        return lax.dynamic_slice_in_dim(array, first_row, row_count, 0)

    tree_factor = jnp.exp(take_rows(tree_max) - take_rows(overall))
    weighted = shared_acc + take_rows(tree_acc) * tree_factor[..., None]
    totals = shared_tot + take_rows(tree_tot) * tree_factor
    share = (
        (weighted / totals[..., None]).astype(jnp.bfloat16).reshape(row_count, heads * head_size)
    )
    attended = lax.all_gather(share, "seq", axis=0, tiled=True)
    mixed = lax.psum_scatter(
        jnp.dot(attended, out_weight, preferred_element_type=jnp.float32),
        "head",
        scatter_dimension=0,
        tiled=True,
    )
    return mixed.astype(jnp.bfloat16)


def solution(mesh):
    placed = (
        P(None, None, "head", None),
        P(None, None, "head", None),
        P(None, None, "head", None),
        P(None, "seq", "head", None),
        P(None, "seq", "head", None),
        P(),
        P(),
        P("head", "seq"),
    )
    return jax.shard_map(
        body, mesh=mesh, in_specs=placed, out_specs=P("head", "seq"), check_vma=False
    )
```

profile of v0, /device:TPU:0, one launch (start us, length us, event | category | flops | bytes accessed | tf_op | source)
XLA Modules:
  0.0 414.5 jit_solution(2779970047454667348)
XLA Ops:
  6.5 145.8 %while.21 = (s32[]{:T(128)}, f32[4,64,32]{1,0,2:T(4,128)S(1)}, f32[4,64,32]{1,0,2:T(4,128)S(1)}, f32[4,64,32,128]{3,2,1,0:T(8,128)}, f32[4,64,32]{1,0,2:T(4,128)...) while((s32[]{:T(128)}, f32[4,64,32]{1,0,2:T(4,128)S(1)}, ...), condition=%wide.region_5.6_spmd.clone, body=%wide.region_0.5_spmd.clone.sunk | while | flops 2289217536 | bytes 81249280 | solution.py:77
  6.6 1.5 dynamic_slice.82
  8.0 0.7 add_compare_fusion.2
  8.7 2.0 constant_dynamic-slice_fusion.9
  10.7 7.2 %fusion.81 = (f32[4,512]{1,0:T(4,128)S(1)}, f32[4,512,2048]{2,1,0:T(8,128)}) fusion(pred[2048]{0:T(1024)(128)(4,1)S(1)} %add_compare_fusion.2, bf16[1,2048,4,128]{3,2,1,0:T(4,128)(2,1)S(1)} %constant_dynamic-slice_fusion.9, bf16[4,64,32,128]{3,2,1,0:T(8,128)(2,1)S(1)} %copy-done, s32[]{:T(128)S(6)} %copy.150), kind=kOutput, calls=%fused_computation.3.clone.1 | convolution fusion | flops 1086322688 | bytes 19408900 | tf_op jit(solution)/shard_map/while/body/eval_jaxpr/kqd,pkd->kqp/dot_general | solution.py:23
  18.2 8.1 %fusion.82 = f32[4,512]{1,0:T(4,128)S(1)} fusion(f32[4,512,2048]{2,1,0:T(8,128)} %get-tuple-element.325, f32[4,512]{1,0:T(4,128)S(1)} %get-tuple-element.324, pred[2048]{0:T(1024)(128)(4,1)S(1)} %add_compare_fusion.2), kind=kLoop, calls=%fused_computation.5.clone.1 | loop fusion | flops 20969472 | bytes 16795648 | tf_op jit(solution)/shard_map/while/body/eval_jaxpr/reduce_sum | solution.py:29
  26.6 0.9 constant_dynamic-slice_fusion.10
  27.5 0.7 fusion.83
  29.4 0.3 fusion.85
  29.8 0.9 constant_dynamic-slice_fusion.11
  30.6 0.4 convolution_bitcast_fusion.2
  31.0 2.0 constant_dynamic-slice_fusion.12
  33.0 7.7 %fusion.86 = f32[64,4,8,128]{3,2,0,1:T(8,128)S(1)} fusion(bf16[1,2048,4,128]{3,2,1,0:T(4,128)(2,1)S(1)} %constant_dynamic-slice_fusion.12, f32[4,512,2048]{2,1,0:T(8,128)} %get-tuple-element.325, f32[4,512]{1,0:T(4,128)S(1)} %get-tuple-element.324, pred[2048]{0:T(1024)(128)(4,1)S(1)} %add_compare_fusion.2), kind=kOutput, calls=%fused_computation.11.clone.1 | convolution fusion | flops 1094713344 | bytes 19933184 | tf_op jit(solution)/shard_map/while/body/eval_jaxpr/kqp,pkd->kqd/dot_general | solution.py:30
  40.7 1.6 bitcast_dynamic-update-slice_fusion.3
  43.0 1.5 dynamic_slice.82
  44.5 0.7 add_compare_fusion.2
  45.2 2.0 constant_dynamic-slice_fusion.9
  47.2 7.2 %fusion.81 = (f32[4,512]{1,0:T(4,128)S(1)}, f32[4,512,2048]{2,1,0:T(8,128)}) fusion(pred[2048]{0:T(1024)(128)(4,1)S(1)} %add_compare_fusion.2, bf16[1,2048,4,128]{3,2,1,0:T(4,128)(2,1)S(1)} %constant_dynamic-slice_fusion.9, bf16[4,64,32,128]{3,2,1,0:T(8,128)(2,1)S(1)} %copy-done, s32[]{:T(128)S(6)} %copy.150), kind=kOutput, calls=%fused_computation.3.clone.1 | convolution fusion | flops 1086322688 | bytes 19408900 | tf_op jit(solution)/shard_map/while/body/eval_jaxpr/kqd,pkd->kqp/dot_general | solution.py:23
  54.7 8.1 %fusion.82 = f32[4,512]{1,0:T(4,128)S(1)} fusion(f32[4,512,2048]{2,1,0:T(8,128)} %get-tuple-element.325, f32[4,512]{1,0:T(4,128)S(1)} %get-tuple-element.324, pred[2048]{0:T(1024)(128)(4,1)S(1)} %add_compare_fusion.2), kind=kLoop, calls=%fused_computation.5.clone.1 | loop fusion | flops 20969472 | bytes 16795648 | tf_op jit(solution)/shard_map/while/body/eval_jaxpr/reduce_sum | solution.py:29
  63.1 0.9 constant_dynamic-slice_fusion.10
  63.9 0.7 fusion.83
  65.9 0.3 fusion.85
  66.2 0.9 constant_dynamic-slice_fusion.11
  67.1 0.4 convolution_bitcast_fusion.2
  67.5 2.0 constant_dynamic-slice_fusion.12
  69.5 7.7 %fusion.86 = f32[64,4,8,128]{3,2,0,1:T(8,128)S(1)} fusion(bf16[1,2048,4,128]{3,2,1,0:T(4,128)(2,1)S(1)} %constant_dynamic-slice_fusion.12, f32[4,512,2048]{2,1,0:T(8,128)} %get-tuple-element.325, f32[4,512]{1,0:T(4,128)S(1)} %get-tuple-element.324, pred[2048]{0:T(1024)(128)(4,1)S(1)} %add_compare_fusion.2), kind=kOutput, calls=%fused_computation.11.clone.1 | convolution fusion | flops 1094713344 | bytes 19933184 | tf_op jit(solution)/shard_map/while/body/eval_jaxpr/kqp,pkd->kqd/dot_general | solution.py:30
  77.1 1.6 bitcast_dynamic-update-slice_fusion.3
  79.5 1.5 dynamic_slice.82
  81.0 0.7 add_compare_fusion.2
  81.7 2.0 constant_dynamic-slice_fusion.9
  83.7 7.2 %fusion.81 = (f32[4,512]{1,0:T(4,128)S(1)}, f32[4,512,2048]{2,1,0:T(8,128)}) fusion(pred[2048]{0:T(1024)(128)(4,1)S(1)} %add_compare_fusion.2, bf16[1,2048,4,128]{3,2,1,0:T(4,128)(2,1)S(1)} %constant_dynamic-slice_fusion.9, bf16[4,64,32,128]{3,2,1,0:T(8,128)(2,1)S(1)} %copy-done, s32[]{:T(128)S(6)} %copy.150), kind=kOutput, calls=%fused_computation.3.clone.1 | convolution fusion | flops 1086322688 | bytes 19408900 | tf_op jit(solution)/shard_map/while/body/eval_jaxpr/kqd,pkd->kqp/dot_general | solution.py:23
  91.2 8.1 %fusion.82 = f32[4,512]{1,0:T(4,128)S(1)} fusion(f32[4,512,2048]{2,1,0:T(8,128)} %get-tuple-element.325, f32[4,512]{1,0:T(4,128)S(1)} %get-tuple-element.324, pred[2048]{0:T(1024)(128)(4,1)S(1)} %add_compare_fusion.2), kind=kLoop, calls=%fused_computation.5.clone.1 | loop fusion | flops 20969472 | bytes 16795648 | tf_op jit(solution)/shard_map/while/body/eval_jaxpr/reduce_sum | solution.py:29
  99.5 0.9 constant_dynamic-slice_fusion.10
  100.4 0.7 fusion.83
  102.4 0.3 fusion.85
  102.7 0.9 constant_dynamic-slice_fusion.11
  103.6 0.4 convolution_bitcast_fusion.2
  104.0 2.0 constant_dynamic-slice_fusion.12
  105.9 7.7 %fusion.86 = f32[64,4,8,128]{3,2,0,1:T(8,128)S(1)} fusion(bf16[1,2048,4,128]{3,2,1,0:T(4,128)(2,1)S(1)} %constant_dynamic-slice_fusion.12, f32[4,512,2048]{2,1,0:T(8,128)} %get-tuple-element.325, f32[4,512]{1,0:T(4,128)S(1)} %get-tuple-element.324, pred[2048]{0:T(1024)(128)(4,1)S(1)} %add_compare_fusion.2), kind=kOutput, calls=%fused_computation.11.clone.1 | convolution fusion | flops 1094713344 | bytes 19933184 | tf_op jit(solution)/shard_map/while/body/eval_jaxpr/kqp,pkd->kqd/dot_general | solution.py:30
  113.6 1.6 bitcast_dynamic-update-slice_fusion.3
  116.0 1.5 dynamic_slice.82
  117.4 0.7 add_compare_fusion.2
  118.1 2.0 constant_dynamic-slice_fusion.9
  120.1 7.2 %fusion.81 = (f32[4,512]{1,0:T(4,128)S(1)}, f32[4,512,2048]{2,1,0:T(8,128)}) fusion(pred[2048]{0:T(1024)(128)(4,1)S(1)} %add_compare_fusion.2, bf16[1,2048,4,128]{3,2,1,0:T(4,128)(2,1)S(1)} %constant_dynamic-slice_fusion.9, bf16[4,64,32,128]{3,2,1,0:T(8,128)(2,1)S(1)} %copy-done, s32[]{:T(128)S(6)} %copy.150), kind=kOutput, calls=%fused_computation.3.clone.1 | convolution fusion | flops 1086322688 | bytes 19408900 | tf_op jit(solution)/shard_map/while/body/eval_jaxpr/kqd,pkd->kqp/dot_general | solution.py:23
  127.6 8.1 %fusion.82 = f32[4,512]{1,0:T(4,128)S(1)} fusion(f32[4,512,2048]{2,1,0:T(8,128)} %get-tuple-element.325, f32[4,512]{1,0:T(4,128)S(1)} %get-tuple-element.324, pred[2048]{0:T(1024)(128)(4,1)S(1)} %add_compare_fusion.2), kind=kLoop, calls=%fused_computation.5.clone.1 | loop fusion | flops 20969472 | bytes 16795648 | tf_op jit(solution)/shard_map/while/body/eval_jaxpr/reduce_sum | solution.py:29
  136.0 0.9 constant_dynamic-slice_fusion.10
  136.9 0.7 fusion.83
  139.2 0.9 constant_dynamic-slice_fusion.11
  140.0 0.4 convolution_bitcast_fusion.2
  140.4 2.0 constant_dynamic-slice_fusion.12
  142.4 7.7 %fusion.86 = f32[64,4,8,128]{3,2,0,1:T(8,128)S(1)} fusion(bf16[1,2048,4,128]{3,2,1,0:T(4,128)(2,1)S(1)} %constant_dynamic-slice_fusion.12, f32[4,512,2048]{2,1,0:T(8,128)} %get-tuple-element.325, f32[4,512]{1,0:T(4,128)S(1)} %get-tuple-element.324, pred[2048]{0:T(1024)(128)(4,1)S(1)} %add_compare_fusion.2), kind=kOutput, calls=%fused_computation.11.clone.1 | convolution fusion | flops 1094713344 | bytes 19933184 | tf_op jit(solution)/shard_map/while/body/eval_jaxpr/kqp,pkd->kqd/dot_general | solution.py:30
  150.1 1.6 bitcast_dynamic-update-slice_fusion.3
  152.6 63.0 %pmax.7 = f32[256,32]{0,1:T(8,128)S(1)} all-reduce(f32[256,32]{0,1:T(8,128)S(1)} %reshape.69), channel_id=1, replica_groups=mesh['seq'=16,'head'=2] {'seq'}, use_global_device_ids=true, to_apply=%region_6.7 | all-reduce | flops 8192 | bytes 65536 | tf_op jit(solution)/shard_map/pmax | solution.py:86
  215.7 0.8 copy.68
  216.6 4.1 %bitcast_multiply_fusion = f32[256,32,128]{2,1,0:T(8,128)} fusion(f32[4,64,32,128]{3,2,1,0:T(8,128)} %get-tuple-element.87, f32[256,32]{1,0:T(8,128)S(1)} %copy.63), kind=kLoop, calls=%fused_computation.55 | loop fusion | flops 1048576 | bytes 8421376 | tf_op jit(solution)/shard_map/mul | solution.py:90
  221.0 48.6 %reduce-scatter.10.cloned.1.call-done = f32[16,32]{1,0:T(8,128)} async-done(((f32[256,32]{1,0:T(8,128)}), f32[16,32]{1,0:T(8,128)}) %reduce-scatter.10.cloned.1.call-update) | async-done | bytes 2064
  269.5 0.8 copy.69
  270.5 74.7 %reduce-scatter.6.cloned.1.call-done = f32[16,32,128]{2,1,0:T(8,128)} async-done(((f32[256,32,128]{2,1,0:T(8,128)}), f32[16,32,128]{2,1,0:T(8,128)}) %reduce-scatter.6.cloned.1.call-update) | async-done | bytes 262160 | tf_op jit(solution)/shard_map/reduce_scatter | solution.py:90
  345.2 1.2 divide_convert_fusion
  346.4 0.7 copy.112
  347.2 40.7 %all-gather.2.cloned.1.call-done = bf16[256,4096]{1,0:T(8,128)(2,1)} async-done(((bf16[16,4096]{1,0:T(8,128)(2,1)}), bf16[256,4096]{1,0:T(8,128)(2,1)}) %all-gather.2.cloned.1.call-update) | async-done | bytes 2097168 | tf_op jit(solution)/shard_map/all_gather | solution.py:105
  387.9 4.9 %fusion.35 = f32[256,512]{1,0:T(8,128)} fusion(bf16[256,4096]{1,0:T(8,128)(2,1)} %all-gather.2.cloned.1.call-done, bf16[4096,512]{1,0:T(8,128)(2,1)} %param.17), kind=kOutput, calls=%fused_computation.63 | convolution fusion | flops 1073741824 | bytes 6815744 | tf_op jit(solution)/shard_map/dot_general | solution.py:107
  392.8 13.5 %reduce-scatter.8.cloned.1.call-done = f32[128,512]{1,0:T(8,128)} async-done(((f32[256,512]{1,0:T(8,128)}), f32[128,512]{1,0:T(8,128)}) %reduce-scatter.8.cloned.1.call-update) | async-done | bytes 262160 | tf_op jit(solution)/shard_map/reduce_scatter | solution.py:106
  406.3 1.6 convert_element_type.19
  (116 shorter events, 11.1 us)
Async XLA Ops:
  6.5 263.0 %reduce-scatter.10.cloned.1.call-start = ((), (), s32[]{:S(2)}) async-start(), calls=%async_computation.6 | async-start | bytes 139264
  6.6 4.2 %copy-start = (bf16[4,64,32,128]{3,2,1,0:T(8,128)(2,1)S(1)}, bf16[4,64,32,128]{3,2,1,0:T(8,128)(2,1)}, u32[]{:S(2)}) copy-start(bf16[4,64,32,128]{3,2,1,0:T(8,128)(2,1)} %get-tuple-element.372) | copy-start | bytes 6291460 | tf_op jit(solution)/shard_map/while
  43.0 4.2 %copy-start = (bf16[4,64,32,128]{3,2,1,0:T(8,128)(2,1)S(1)}, bf16[4,64,32,128]{3,2,1,0:T(8,128)(2,1)}, u32[]{:S(2)}) copy-start(bf16[4,64,32,128]{3,2,1,0:T(8,128)(2,1)} %get-tuple-element.372) | copy-start | bytes 6291460 | tf_op jit(solution)/shard_map/while
  79.5 4.2 %copy-start = (bf16[4,64,32,128]{3,2,1,0:T(8,128)(2,1)S(1)}, bf16[4,64,32,128]{3,2,1,0:T(8,128)(2,1)}, u32[]{:S(2)}) copy-start(bf16[4,64,32,128]{3,2,1,0:T(8,128)(2,1)} %get-tuple-element.372) | copy-start | bytes 6291460 | tf_op jit(solution)/shard_map/while
  116.0 4.2 %copy-start = (bf16[4,64,32,128]{3,2,1,0:T(8,128)(2,1)S(1)}, bf16[4,64,32,128]{3,2,1,0:T(8,128)(2,1)}, u32[]{:S(2)}) copy-start(bf16[4,64,32,128]{3,2,1,0:T(8,128)(2,1)} %get-tuple-element.372) | copy-start | bytes 6291460 | tf_op jit(solution)/shard_map/while
  216.5 128.7 %reduce-scatter.6.cloned.1.call-start = ((), (), s32[]{:S(2)}) async-start(), calls=%async_computation.3 | async-start | bytes 4456448 | tf_op jit(solution)/shard_map/reduce_scatter | solution.py:90
  220.8 167.1 %all-gather.2.cloned.1.call-start = ((), (), s32[]{:S(2)}) async-start(), calls=%async_computation.4 | async-start | bytes 2228224 | tf_op jit(solution)/shard_map/all_gather | solution.py:105
  347.2 59.1 %reduce-scatter.8.cloned.1.call-start = ((), (), s32[]{:S(2)}) async-start(), calls=%async_computation.5 | async-start | bytes 786432 | tf_op jit(solution)/shard_map/reduce_scatter | solution.py:106
Sparse Core Ops, SparseCore 0:
  216.6 52.8 reduce-scatter.9
  273.4 71.7 reduce-scatter.5
  347.4 40.4 all-gather.1
  392.9 13.3 reduce-scatter.7
where the time goes:
time: 416 us; the launch traced here: 414 us
  waiting for transfers between devices  178 us (43%)
  matrix products  71.1 us (17%)
  blocking collectives  63 us (15%)
  local copies, waits for them, and re-layouts  46 us (11%)
  other arithmetic  42.7 us (10%)
  between operations  13.2 us (3%)
    reduce_scatter x1, waiting for transfers between devices, body(): lax.psum_scatter(cache_acc * factor[..., None], 'seq', scatter_dimension=...  74.7 us
    pmax x1, blocking collectives, body(): overall = lax.pmax(cache_max, 'seq')  63 us
    unnamed x5, waiting for transfers between devices  48.6 us
    all_gather x1, waiting for transfers between devices, body(): attended = lax.all_gather(share, 'seq', axis=0, tiled=True)  40.7 us
    reduce_sum x8, other arithmetic, partial_scores(): totals = jnp.sum(weights, axis=-1)  32.9 us
    dot_general x8, matrix products, partial_scores(): jnp.einsum('kqp,pkd->kqd', weights.astype(jnp.bfloat16), values, preferre...  32.1 us
    dot_general x8, matrix products, partial_scores(): jnp.einsum('kqd,pkd->kqp', query_rows, keys, preferred_element_type=jnp.f...  30 us
    dynamic_slice x20, local copies, waits for them, and re-layouts, body(): lax.map(one_request, (queries, new_keys, new_values, cache_keys, cache_va...  28.8 us
  transfers between devices with their start and end apart: 4, of which 4 were waited for; matrix products, arithmetic and copies ran while one was open for 1% of the time, Pallas kernels for 0%

commit v1 on v0

--- a/solution.py
+++ b/solution.py
@@ -102,7 +102,16 @@
     share = (
         (weighted / totals[..., None]).astype(jnp.bfloat16).reshape(row_count, heads * head_size)
     )
-    attended = lax.all_gather(share, "seq", axis=0, tiled=True)
+    files_arrange = lambda frame, mesh_name: jnp.concatenate(
+        lax.all_to_all(
+            jnp.stack([frame for _ in range(lax.axis_size(mesh_name))], axis=0),
+            axis_name=mesh_name,
+            split_axis=0,
+            concat_axis=0,
+        ),
+        axis=0,
+    )
+    attended = files_arrange(share, "seq")
     mixed = lax.psum_scatter(
         jnp.dot(attended, out_weight, preferred_element_type=jnp.float32),
         "head",

time: 416 us -> 424 us (1.019)
  blocking collectives: 63 us -> 114 us
  waiting for transfers between devices: 178 us -> 139 us
    all_to_all x0 -> x1, blocking collectives: none -> 50.7 us  [body(): lax.all_to_all(jnp.stack([frame for _ in range(lax.axis_size(mesh_name))]...]
    all_gather x1 -> x0, waiting for transfers between devices: 40.7 us -> none  [body(): attended = lax.all_gather(share, 'seq', axis=0, tiled=True)]
    unnamed x5 -> x4, waiting for transfers between devices: 48.6 us -> 48.6 us
  transfers between devices with their start and end apart: 4 -> 3, of which waited for: 4 -> 3; matrix products, arithmetic and copies ran while one was open for 1% -> 1% of each run, Pallas kernels for 0% -> 0%
where the time goes in v1:
time: 424 us; the launch traced here: 423 us
  waiting for transfers between devices  139 us (33%)
  blocking collectives  114 us (27%)
  matrix products  68.3 us (16%)
  local copies, waits for them, and re-layouts  45.6 us (11%)
  other arithmetic  42.9 us (10%)
  between operations  13.2 us (3%)
    reduce_scatter x1, waiting for transfers between devices, body(): lax.psum_scatter(cache_acc * factor[..., None], 'seq', scatter_dimension=...  74.7 us
    pmax x1, blocking collectives, body(): overall = lax.pmax(cache_max, 'seq')  63 us
    all_to_all x1, blocking collectives, body(): lax.all_to_all(jnp.stack([frame for _ in range(lax.axis_size(mesh_name))]...  50.7 us
    unnamed x4, waiting for transfers between devices  48.6 us
    reduce_sum x8, other arithmetic, partial_scores(): totals = jnp.sum(weights, axis=-1)  32.9 us
    dot_general x8, matrix products, partial_scores(): jnp.einsum('kqp,pkd->kqd', weights.astype(jnp.bfloat16), values, preferre...  32.1 us
    dot_general x8, matrix products, partial_scores(): jnp.einsum('kqd,pkd->kqp', query_rows, keys, preferred_element_type=jnp.f...  30 us
    dynamic_slice x20, local copies, waits for them, and re-layouts, body(): lax.map(one_request, (queries, new_keys, new_values, cache_keys, cache_va...  28.8 us
  transfers between devices with their start and end apart: 3, of which 3 were waited for; matrix products, arithmetic and copies ran while one was open for 1% of the time, Pallas kernels for 0%

profile of v1, /device:TPU:0, one launch (start us, length us, event | category | flops | bytes accessed | tf_op | source)
XLA Modules:
  0.0 423.1 jit_solution(15765110066268389310)
XLA Ops:
  6.5 145.8 %while.21 = (s32[]{:T(128)}, f32[4,64,32]{1,0,2:T(4,128)S(1)}, f32[4,64,32]{1,0,2:T(4,128)S(1)}, f32[4,64,32,128]{3,2,1,0:T(8,128)}, f32[4,64,32]{1,0,2:T(4,128)...) while((s32[]{:T(128)}, f32[4,64,32]{1,0,2:T(4,128)S(1)}, ...), condition=%wide.region_5.6_spmd.clone, body=%wide.region_0.5_spmd.clone.sunk | while | flops 2289217536 | bytes 81249280 | solution.py:77
  6.6 1.5 dynamic_slice.82
  8.0 0.7 add_compare_fusion.2
  8.7 2.0 constant_dynamic-slice_fusion.9
  10.7 7.2 %fusion.81 = (f32[4,512]{1,0:T(4,128)S(1)}, f32[4,512,2048]{2,1,0:T(8,128)}) fusion(pred[2048]{0:T(1024)(128)(4,1)S(1)} %add_compare_fusion.2, bf16[1,2048,4,128]{3,2,1,0:T(4,128)(2,1)S(1)} %constant_dynamic-slice_fusion.9, bf16[4,64,32,128]{3,2,1,0:T(8,128)(2,1)S(1)} %copy-done, s32[]{:T(128)S(6)} %copy.150), kind=kOutput, calls=%fused_computation.3.clone.1 | convolution fusion | flops 1086322688 | bytes 19408900 | tf_op jit(solution)/shard_map/while/body/eval_jaxpr/kqd,pkd->kqp/dot_general | solution.py:23
  18.2 8.1 %fusion.82 = f32[4,512]{1,0:T(4,128)S(1)} fusion(f32[4,512,2048]{2,1,0:T(8,128)} %get-tuple-element.325, f32[4,512]{1,0:T(4,128)S(1)} %get-tuple-element.324, pred[2048]{0:T(1024)(128)(4,1)S(1)} %add_compare_fusion.2), kind=kLoop, calls=%fused_computation.5.clone.1 | loop fusion | flops 20969472 | bytes 16795648 | tf_op jit(solution)/shard_map/while/body/eval_jaxpr/reduce_sum | solution.py:29
  26.6 0.9 constant_dynamic-slice_fusion.10
  27.5 0.7 fusion.83
  29.4 0.3 fusion.85
  29.8 0.9 constant_dynamic-slice_fusion.11
  30.6 0.4 convolution_bitcast_fusion.2
  31.0 2.0 constant_dynamic-slice_fusion.12
  33.0 7.7 %fusion.86 = f32[64,4,8,128]{3,2,0,1:T(8,128)S(1)} fusion(bf16[1,2048,4,128]{3,2,1,0:T(4,128)(2,1)S(1)} %constant_dynamic-slice_fusion.12, f32[4,512,2048]{2,1,0:T(8,128)} %get-tuple-element.325, f32[4,512]{1,0:T(4,128)S(1)} %get-tuple-element.324, pred[2048]{0:T(1024)(128)(4,1)S(1)} %add_compare_fusion.2), kind=kOutput, calls=%fused_computation.11.clone.1 | convolution fusion | flops 1094713344 | bytes 19933184 | tf_op jit(solution)/shard_map/while/body/eval_jaxpr/kqp,pkd->kqd/dot_general | solution.py:30
  40.7 1.6 bitcast_dynamic-update-slice_fusion.3
  43.0 1.5 dynamic_slice.82
  44.5 0.7 add_compare_fusion.2
  45.2 2.0 constant_dynamic-slice_fusion.9
  47.2 7.2 %fusion.81 = (f32[4,512]{1,0:T(4,128)S(1)}, f32[4,512,2048]{2,1,0:T(8,128)}) fusion(pred[2048]{0:T(1024)(128)(4,1)S(1)} %add_compare_fusion.2, bf16[1,2048,4,128]{3,2,1,0:T(4,128)(2,1)S(1)} %constant_dynamic-slice_fusion.9, bf16[4,64,32,128]{3,2,1,0:T(8,128)(2,1)S(1)} %copy-done, s32[]{:T(128)S(6)} %copy.150), kind=kOutput, calls=%fused_computation.3.clone.1 | convolution fusion | flops 1086322688 | bytes 19408900 | tf_op jit(solution)/shard_map/while/body/eval_jaxpr/kqd,pkd->kqp/dot_general | solution.py:23
  54.7 8.1 %fusion.82 = f32[4,512]{1,0:T(4,128)S(1)} fusion(f32[4,512,2048]{2,1,0:T(8,128)} %get-tuple-element.325, f32[4,512]{1,0:T(4,128)S(1)} %get-tuple-element.324, pred[2048]{0:T(1024)(128)(4,1)S(1)} %add_compare_fusion.2), kind=kLoop, calls=%fused_computation.5.clone.1 | loop fusion | flops 20969472 | bytes 16795648 | tf_op jit(solution)/shard_map/while/body/eval_jaxpr/reduce_sum | solution.py:29
  63.1 0.9 constant_dynamic-slice_fusion.10
  63.9 0.7 fusion.83
  65.9 0.3 fusion.85
  66.2 0.9 constant_dynamic-slice_fusion.11
  67.1 0.4 convolution_bitcast_fusion.2
  67.5 2.0 constant_dynamic-slice_fusion.12
  69.5 7.7 %fusion.86 = f32[64,4,8,128]{3,2,0,1:T(8,128)S(1)} fusion(bf16[1,2048,4,128]{3,2,1,0:T(4,128)(2,1)S(1)} %constant_dynamic-slice_fusion.12, f32[4,512,2048]{2,1,0:T(8,128)} %get-tuple-element.325, f32[4,512]{1,0:T(4,128)S(1)} %get-tuple-element.324, pred[2048]{0:T(1024)(128)(4,1)S(1)} %add_compare_fusion.2), kind=kOutput, calls=%fused_computation.11.clone.1 | convolution fusion | flops 1094713344 | bytes 19933184 | tf_op jit(solution)/shard_map/while/body/eval_jaxpr/kqp,pkd->kqd/dot_general | solution.py:30
  77.1 1.6 bitcast_dynamic-update-slice_fusion.3
  79.5 1.5 dynamic_slice.82
  81.0 0.7 add_compare_fusion.2
  81.7 2.0 constant_dynamic-slice_fusion.9
  83.7 7.2 %fusion.81 = (f32[4,512]{1,0:T(4,128)S(1)}, f32[4,512,2048]{2,1,0:T(8,128)}) fusion(pred[2048]{0:T(1024)(128)(4,1)S(1)} %add_compare_fusion.2, bf16[1,2048,4,128]{3,2,1,0:T(4,128)(2,1)S(1)} %constant_dynamic-slice_fusion.9, bf16[4,64,32,128]{3,2,1,0:T(8,128)(2,1)S(1)} %copy-done, s32[]{:T(128)S(6)} %copy.150), kind=kOutput, calls=%fused_computation.3.clone.1 | convolution fusion | flops 1086322688 | bytes 19408900 | tf_op jit(solution)/shard_map/while/body/eval_jaxpr/kqd,pkd->kqp/dot_general | solution.py:23
  91.2 8.1 %fusion.82 = f32[4,512]{1,0:T(4,128)S(1)} fusion(f32[4,512,2048]{2,1,0:T(8,128)} %get-tuple-element.325, f32[4,512]{1,0:T(4,128)S(1)} %get-tuple-element.324, pred[2048]{0:T(1024)(128)(4,1)S(1)} %add_compare_fusion.2), kind=kLoop, calls=%fused_computation.5.clone.1 | loop fusion | flops 20969472 | bytes 16795648 | tf_op jit(solution)/shard_map/while/body/eval_jaxpr/reduce_sum | solution.py:29
  99.5 0.9 constant_dynamic-slice_fusion.10
  100.4 0.7 fusion.83
  102.4 0.3 fusion.85
  102.7 0.9 constant_dynamic-slice_fusion.11
  103.6 0.4 convolution_bitcast_fusion.2
  104.0 2.0 constant_dynamic-slice_fusion.12
  105.9 7.7 %fusion.86 = f32[64,4,8,128]{3,2,0,1:T(8,128)S(1)} fusion(bf16[1,2048,4,128]{3,2,1,0:T(4,128)(2,1)S(1)} %constant_dynamic-slice_fusion.12, f32[4,512,2048]{2,1,0:T(8,128)} %get-tuple-element.325, f32[4,512]{1,0:T(4,128)S(1)} %get-tuple-element.324, pred[2048]{0:T(1024)(128)(4,1)S(1)} %add_compare_fusion.2), kind=kOutput, calls=%fused_computation.11.clone.1 | convolution fusion | flops 1094713344 | bytes 19933184 | tf_op jit(solution)/shard_map/while/body/eval_jaxpr/kqp,pkd->kqd/dot_general | solution.py:30
  113.6 1.6 bitcast_dynamic-update-slice_fusion.3
  116.0 1.5 dynamic_slice.82
  117.4 0.7 add_compare_fusion.2
  118.1 2.0 constant_dynamic-slice_fusion.9
  120.1 7.2 %fusion.81 = (f32[4,512]{1,0:T(4,128)S(1)}, f32[4,512,2048]{2,1,0:T(8,128)}) fusion(pred[2048]{0:T(1024)(128)(4,1)S(1)} %add_compare_fusion.2, bf16[1,2048,4,128]{3,2,1,0:T(4,128)(2,1)S(1)} %constant_dynamic-slice_fusion.9, bf16[4,64,32,128]{3,2,1,0:T(8,128)(2,1)S(1)} %copy-done, s32[]{:T(128)S(6)} %copy.150), kind=kOutput, calls=%fused_computation.3.clone.1 | convolution fusion | flops 1086322688 | bytes 19408900 | tf_op jit(solution)/shard_map/while/body/eval_jaxpr/kqd,pkd->kqp/dot_general | solution.py:23
  127.6 8.1 %fusion.82 = f32[4,512]{1,0:T(4,128)S(1)} fusion(f32[4,512,2048]{2,1,0:T(8,128)} %get-tuple-element.325, f32[4,512]{1,0:T(4,128)S(1)} %get-tuple-element.324, pred[2048]{0:T(1024)(128)(4,1)S(1)} %add_compare_fusion.2), kind=kLoop, calls=%fused_computation.5.clone.1 | loop fusion | flops 20969472 | bytes 16795648 | tf_op jit(solution)/shard_map/while/body/eval_jaxpr/reduce_sum | solution.py:29
  136.0 0.9 constant_dynamic-slice_fusion.10
  136.9 0.7 fusion.83
  138.8 0.3 fusion.85
  139.2 0.9 constant_dynamic-slice_fusion.11
  140.0 0.4 convolution_bitcast_fusion.2
  140.4 2.0 constant_dynamic-slice_fusion.12
  142.4 7.7 %fusion.86 = f32[64,4,8,128]{3,2,0,1:T(8,128)S(1)} fusion(bf16[1,2048,4,128]{3,2,1,0:T(4,128)(2,1)S(1)} %constant_dynamic-slice_fusion.12, f32[4,512,2048]{2,1,0:T(8,128)} %get-tuple-element.325, f32[4,512]{1,0:T(4,128)S(1)} %get-tuple-element.324, pred[2048]{0:T(1024)(128)(4,1)S(1)} %add_compare_fusion.2), kind=kOutput, calls=%fused_computation.11.clone.1 | convolution fusion | flops 1094713344 | bytes 19933184 | tf_op jit(solution)/shard_map/while/body/eval_jaxpr/kqp,pkd->kqd/dot_general | solution.py:30
  150.1 1.6 bitcast_dynamic-update-slice_fusion.3
  152.6 63.0 %pmax.7 = f32[256,32]{0,1:T(8,128)S(1)} all-reduce(f32[256,32]{0,1:T(8,128)S(1)} %reshape.71), channel_id=1, replica_groups=mesh['seq'=16,'head'=2] {'seq'}, use_global_device_ids=true, to_apply=%region_6.7 | all-reduce | flops 8192 | bytes 65536 | tf_op jit(solution)/shard_map/pmax | solution.py:86
  215.7 0.8 copy.68
  216.6 4.1 bitcast_multiply_fusion
  221.0 48.6 %reduce-scatter.10.cloned.1.call-done = f32[16,32]{1,0:T(8,128)} async-done(((f32[256,32]{1,0:T(8,128)}), f32[16,32]{1,0:T(8,128)}) %reduce-scatter.10.cloned.1.call-update) | async-done | bytes 2064
  269.5 0.8 copy.69
  270.5 74.7 %reduce-scatter.6.cloned.1.call-done = f32[16,32,128]{2,1,0:T(8,128)} async-done(((f32[256,32,128]{2,1,0:T(8,128)}), f32[16,32,128]{2,1,0:T(8,128)}) %reduce-scatter.6.cloned.1.call-update) | async-done | bytes 262160 | tf_op jit(solution)/shard_map/reduce_scatter | solution.py:90
  345.2 1.4 divide_convert_fusion
  346.9 50.7 %all_to_all.5 = bf16[16,16,4096]{2,1,0:T(8,128)(2,1)S(1)} all-to-all(bf16[16,16,4096]{2,1,0:T(8,128)(2,1)S(1)} %stack.3), channel_id=1, replica_groups=mesh['seq'=16,'head'=2] {'seq'}, dimensions={0} | all-to-all | bytes 4194304 | tf_op jit(solution)/shard_map/all_to_all | solution.py:106
  397.6 2.0 fusion.35
  399.7 15.2 %reduce-scatter.8.cloned.1.call-done = f32[128,512]{1,0:T(8,128)} async-done(((f32[256,512]{1,0:T(8,128)}), f32[128,512]{1,0:T(8,128)}) %reduce-scatter.8.cloned.1.call-update) | async-done | bytes 262160 | tf_op jit(solution)/shard_map/reduce_scatter | solution.py:115
  414.9 1.6 convert_element_type.19
  (117 shorter events, 11.0 us)
Async XLA Ops:
  6.5 263.0 %reduce-scatter.10.cloned.1.call-start = ((), (), s32[]{:S(2)}) async-start(), calls=%async_computation.6 | async-start | bytes 139264
  6.6 4.2 copy-start
  43.0 4.2 copy-start
  79.5 4.2 copy-start
  116.0 4.2 copy-start
  216.5 128.7 %reduce-scatter.6.cloned.1.call-start = ((), (), s32[]{:S(2)}) async-start(), calls=%async_computation.4 | async-start | bytes 4456448 | tf_op jit(solution)/shard_map/reduce_scatter | solution.py:90
  220.8 194.1 %reduce-scatter.8.cloned.1.call-start = ((), (), s32[]{:S(2)}) async-start(), calls=%async_computation.5 | async-start | bytes 786432 | tf_op jit(solution)/shard_map/reduce_scatter | solution.py:115
  345.2 52.4 %copy-start.1 = (bf16[4096,512]{1,0:T(8,128)(2,1)S(1)}, bf16[4096,512]{1,0:T(8,128)(2,1)}, u32[]{:S(2)}) copy-start(bf16[4096,512]{1,0:T(8,128)(2,1)} %param.17) | copy-start | bytes 12582916
Sparse Core Ops, SparseCore 0:
  216.6 52.8 reduce-scatter.9
  273.4 71.7 reduce-scatter.5
  399.8 15.0 reduce-scatter.7
